TPU v7x, 32 devices: a whole 2x2x4 slice. The times are simulated.
32 devices in a mesh: grp: 2 (over x), comp: 16 (over z, y, core).
Axes of the slice: x: 2, y: 2, z: 4, core: 2. Of those that a mesh axis runs over, the one named last changes fastest.
Arguments:
- spectrum: float32 [1152, 96, 128], P(None, ('grp', 'comp')), parts along dimension 1, may hold values from 0.04 to 14, as said below
- sea_mask: int32 [96, 128], P(('grp', 'comp')), parts along dimension 0, may hold values 0 or 1
- ice_mask: int32 [96, 128], P(('grp', 'comp')), parts along dimension 0, may hold values 0 or 1
- wind: float32 [96, 128], P(('grp', 'comp')), parts along dimension 0, may hold values from 0.2 to 1
- source_matrix: bfloat16 [1152, 1152], replicated, may hold values from -0.1875 to 0.1875
Outputs:
- evolved: float32 [1152, 96, 128], P(None, ('grp', 'comp')), parts along dimension 1
There are 2 independent parts, one for each index of `grp`. A program takes and returns all parts, laid end to end along the dimension named above; an argument that names none is the same for every part. Nothing has to cross between parts.
Inputs may be any that keep to these rules, and one draw needn't show every extreme that they name: `spectrum`: positive spectral densities.
All inputs are finite; a program needn't handle non-finite values. No bound on the sum of `sea_mask` or of `ice_mask` on one device may be relied on, other than what follows from the above.
Results may differ from a plain program's by a relative error of at most 0.0014.
Values sent between devices are 32-bit elements; how exact they have to be, the bound alone decides.
A program may use at most 64 MiB of HBM per device.

v0:
```python
import jax
import jax.numpy as jnp
from jax import lax
from jax.sharding import PartitionSpec as P

NDIR = 36
NFREQ = 32
K = 1152
STEPS = 2
SUBSTEPS = 3
SRC_SUB = 3


source_rate = 0.5
damping = 0.5


def extended(shard, sides, width):
    for axis, dim in sides:
        size, length = (lax.axis_size(axis), shard.shape[dim])
        up = [(i, (i + 1) % size) for i in range(size - 1)]
        down = [(j, i) for i, j in up]
        last = lax.slice_in_dim(shard, length - width, length, axis=dim)
        leading = lax.slice_in_dim(shard, 0, width, axis=dim)
        before = lax.ppermute(last, axis, up)
        after = lax.ppermute(leading, axis, down)
        shard = jnp.concatenate([before, shard, after], axis=dim)
    return shard


def courant(comp_index):
    direction = (comp_index % NDIR).astype(jnp.float32)
    frequency = (comp_index // NDIR).astype(jnp.float32)
    angles = 2.0 * jnp.pi * (direction + 0.5) / NDIR
    speeds = 0.6 * (0.35 + 0.65 * (NFREQ - 1 - frequency) / (NFREQ - 1))
    return ((speeds * jnp.cos(angles))[:, None, None], (speeds * jnp.sin(angles))[:, None, None])


def advance(spectra, courant_x, courant_y):
    western = jnp.roll(spectra, 1, axis=2)
    eastern = jnp.roll(spectra, -1, axis=2)
    zero_row = jnp.zeros_like(spectra[:, :1])
    southern = jnp.concatenate([zero_row, spectra[:, :-1]], axis=1)
    northern = jnp.concatenate([spectra[:, 1:], zero_row], axis=1)
    staying = 1.0 - jnp.abs(courant_x) - jnp.abs(courant_y)
    return (
        staying * spectra
        + jnp.maximum(courant_x, 0.0) * western
        + jnp.maximum(-courant_x, 0.0) * eastern
        + jnp.maximum(courant_y, 0.0) * southern
        + jnp.maximum(-courant_y, 0.0) * northern
    )


def sources(spectra, sea, wind, source_matrix):
    layout_shape = spectra.shape
    flattened = spectra.reshape(layout_shape[0], -1)
    sea_flat = sea.reshape(1, -1)
    wind_flat = wind.reshape(1, -1)
    for source_step in range(SRC_SUB):
        rounded = flattened.astype(jnp.bfloat16)
        growth = jnp.dot(source_matrix, rounded, preferred_element_type=jnp.float32)
        energy = jnp.mean(flattened * flattened, axis=0, keepdims=True)
        flattened = (
            sea_flat * (flattened + source_rate * wind_flat * growth) / (1.0 + damping * energy)
        )
    return flattened.reshape(layout_shape)


def on_device(spectrum, sea_mask, ice_mask, wind, source_matrix):
    sea_local = sea_mask.astype(jnp.float32)
    thaw = (1.0 - 0.5 * ice_mask.astype(jnp.float32))[None]
    spectra = spectrum
    courant_x, courant_y = courant(jnp.arange(K, dtype=jnp.int32))
    for outer_step in range(STEPS):
        for inner_step in range(SUBSTEPS):
            widened = extended(spectra, (("comp", 1),), 1)
            spectra = sea_local[None] * advance(widened, courant_x, courant_y)[:, 1:-1]
        spectra = sources(spectra, sea_local, wind, source_matrix) * thaw
    return spectra


def solution(mesh):
    return jax.shard_map(
        on_device,
        mesh=mesh,
        in_specs=(
            P(None, ("grp", "comp"), None),
            P(("grp", "comp"), None),
            P(("grp", "comp"), None),
            P(("grp", "comp"), None),
            P(),
        ),
        out_specs=P(None, ("grp", "comp"), None),
        check_vma=False,
    )
```

profile of v0, /device:TPU:1, one launch (start us, length us, event | category | flops | bytes accessed | tf_op | source)
XLA Modules:
  0.0 165.9 jit_solution(6611848075324589240)
XLA Ops:
  0.0 1.5 fusion.134
  1.5 4.7 %collective-permute-start = (f32[1152,1,128]{2,0,1:T(8,128)S(1)}, f32[1152,1,128]{2,0,1:T(8,128)S(1)}, u32[]{:S(2)}, u32[]{:S(2)}) collective-permute-start(f32[1152,1,128]{2,0,1:T(8,128)S(1)} %get-tuple-element.43), channel_id=1, source_target_pairs={{0,1},{1,2},{2,3},{3,4},{4,5},{5,6},{6,7},{7,8},{8,9},{9,10},{10,1... | collective-permute-start | bytes 1769480 | tf_op jit(solution)/shard_map/ppermute | solution.py:25
  6.2 1.9 %collective-permute-start.1 = (f32[1152,1,128]{2,0,1:T(8,128)S(1)}, f32[1152,1,128]{2,0,1:T(8,128)S(1)}, u32[]{:S(2)}, u32[]{:S(2)}) collective-permute-start(f32[1152,1,128]{2,0,1:T(8,128)S(1)} %get-tuple-element.44), channel_id=1, source_target_pairs={{1,0},{2,1},{3,2},{4,3},{5,4},{6,5},{7,6},{8,7},{9,8},{10,9},{11,1... | collective-permute-start | bytes 1769480 | tf_op jit(solution)/shard_map/ppermute | solution.py:26
  8.3 11.0 %collective-permute-done = f32[1152,1,128]{2,0,1:T(8,128)S(1)} collective-permute-done((f32[1152,1,128]{2,0,1:T(8,128)S(1)}, f32[1152,1,128]{2,0,1:T(8,128)S(1)}, u32[]{:S(2)}, u32[]{:S(2)}) %collective-permute-start) | collective-permute-done | bytes 589856 | tf_op jit(solution)/shard_map/ppermute | solution.py:25
  19.5 1.0 fusion.128
  20.5 1.0 fusion.127
  21.4 2.1 %fusion.82 = f32[1152,3,128]{2,0,1:T(8,128)S(1)} fusion(f32[1152,1,128]{2,0,1:T(8,128)S(1)} %collective-permute-done.1, f32[1152,3,128]{2,0,1:T(8,128)S(1)} %copy-done.1, f32[1152,1,128]{2,0,1:T(8,128)S(1)} %collective-permute-done, f32[1152,5,1]{2,0,1:T(8,128)S(1)} %get-tuple-element.30, f32[1152,5,127]{2,0,1:T(8,128)S(1)} %get-tuple-element.32, ...), kind=kLoop, calls=%fused_computation.129 | loop fusion | flops 9289728 | bytes 12410880 | tf_op jit(solution)/shard_map/mul | solution.py:78
  23.6 4.4 %collective-permute-start.2 = (f32[1152,1,128]{2,0,1:T(8,128)S(1)}, f32[1152,1,128]{2,0,1:T(8,128)S(1)}, u32[]{:S(2)}, u32[]{:S(2)}) collective-permute-start(f32[1152,1,128]{2,0,1:T(8,128)S(1)} %get-tuple-element.41), channel_id=1, source_target_pairs={{0,1},{1,2},{2,3},{3,4},{4,5},{5,6},{6,7},{7,8},{8,9},{9,10},{10,1... | collective-permute-start | bytes 1769480 | tf_op jit(solution)/shard_map/ppermute | solution.py:25
  28.0 1.9 %collective-permute-start.3 = (f32[1152,1,128]{2,0,1:T(8,128)S(1)}, f32[1152,1,128]{2,0,1:T(8,128)S(1)}, u32[]{:S(2)}, u32[]{:S(2)}) collective-permute-start(f32[1152,1,128]{2,0,1:T(8,128)S(1)} %get-tuple-element.42), channel_id=1, source_target_pairs={{1,0},{2,1},{3,2},{4,3},{5,4},{6,5},{7,6},{8,7},{9,8},{10,9},{11,1... | collective-permute-start | bytes 1769480 | tf_op jit(solution)/shard_map/ppermute | solution.py:26
  30.0 11.2 %collective-permute-done.2 = f32[1152,1,128]{2,0,1:T(8,128)S(1)} collective-permute-done((f32[1152,1,128]{2,0,1:T(8,128)S(1)}, f32[1152,1,128]{2,0,1:T(8,128)S(1)}, u32[]{:S(2)}, u32[]{:S(2)}) %collective-permute-start.2) | collective-permute-done | bytes 589856 | tf_op jit(solution)/shard_map/ppermute | solution.py:25
  41.3 1.0 fusion.126
  42.3 1.0 fusion.125
  43.3 2.1 %fusion.71 = f32[1152,3,128]{2,0,1:T(8,128)S(1)} fusion(f32[1152,1,128]{2,0,1:T(8,128)S(1)} %collective-permute-done.3, f32[1152,3,128]{2,0,1:T(8,128)S(1)} %fusion.82, f32[1152,1,128]{2,0,1:T(8,128)S(1)} %collective-permute-done.2, f32[1152,5,1]{2,0,1:T(8,128)S(1)} %get-tuple-element.26, f32[1152,5,127]{2,0,1:T(8,128)S(1)} %get-tuple-element.28, ...), kind=kLoop, calls=%fused_computation.111 | loop fusion | flops 9289728 | bytes 12410880 | tf_op jit(solution)/shard_map/mul | solution.py:78
  45.5 4.4 %collective-permute-start.4 = (f32[1152,1,128]{2,0,1:T(8,128)S(1)}, f32[1152,1,128]{2,0,1:T(8,128)S(1)}, u32[]{:S(2)}, u32[]{:S(2)}) collective-permute-start(f32[1152,1,128]{2,0,1:T(8,128)S(1)} %get-tuple-element.39), channel_id=1, source_target_pairs={{0,1},{1,2},{2,3},{3,4},{4,5},{5,6},{6,7},{7,8},{8,9},{9,10},{10,1... | collective-permute-start | bytes 1769480 | tf_op jit(solution)/shard_map/ppermute | solution.py:25
  49.9 2.1 %collective-permute-start.5 = (f32[1152,1,128]{2,0,1:T(8,128)S(1)}, f32[1152,1,128]{2,0,1:T(8,128)S(1)}, u32[]{:S(2)}, u32[]{:S(2)}) collective-permute-start(f32[1152,1,128]{2,0,1:T(8,128)S(1)} %get-tuple-element.40), channel_id=1, source_target_pairs={{1,0},{2,1},{3,2},{4,3},{5,4},{6,5},{7,6},{8,7},{9,8},{10,9},{11,1... | collective-permute-start | bytes 1769480 | tf_op jit(solution)/shard_map/ppermute | solution.py:26
  52.0 11.0 %collective-permute-done.4 = f32[1152,1,128]{2,0,1:T(8,128)S(1)} collective-permute-done((f32[1152,1,128]{2,0,1:T(8,128)S(1)}, f32[1152,1,128]{2,0,1:T(8,128)S(1)}, u32[]{:S(2)}, u32[]{:S(2)}) %collective-permute-start.4) | collective-permute-done | bytes 589856 | tf_op jit(solution)/shard_map/ppermute | solution.py:25
  63.2 1.0 fusion.124
  64.2 1.0 fusion.123
  65.1 3.0 %multiply_reduce_fusion.5 = (f32[3,128]{1,0:T(4,128)S(1)}, f32[1152,3,128]{2,0,1:T(8,128)}) fusion(f32[1152,1,128]{2,0,1:T(8,128)S(1)} %collective-permute-done.5, f32[1152,3,128]{2,0,1:T(8,128)S(1)} %fusion.71, f32[1152]{0:T(1024)S(1)} %get-tuple-element.55, f32[1152,1,128]{2,0,1:T(8,128)S(1)} %collective-permute-done.4, f32[1152]{0:T(1024)S(1)} %get-tuple-element.58, ...), kind=kLoop, calls=%fused_computation.153 | loop fusion | flops 10174080 | bytes 12412416 | tf_op jit(solution)/shard_map/reduce_sum | solution.py:63
  68.1 2.8 %copy.6 = f32[1152,3,128]{0,2,1:T(8,128)} copy(f32[1152,3,128]{2,0,1:T(8,128)} %get-tuple-element.8) | data formatting | bytes 3538944 | tf_op jit(solution)/shard_map/mul | solution.py:78
  70.9 1.7 %bitcast_convert_fusion.1 = bf16[1152,384]{0,1:T(8,128)(2,1)S(1)} fusion(f32[1152,3,128]{0,2,1:T(8,128)} %copy.6), kind=kLoop, calls=%fused_computation.147 | loop fusion | flops 442368 | bytes 2654208 | tf_op jit(solution)/shard_map/convert_element_type | solution.py:61
  72.9 1.7 %multiply_reduce_fusion.4 = (f32[384]{0:T(512)S(1)}, f32[1152,384]{0,1:T(8,128)S(1)}) fusion(f32[384]{0:T(512)S(1)} %add_bitcast_fusion.1, f32[1152,384]{0,1:T(8,128)S(1)} %bitcast.70, bf16[1152,384]{0,1:T(8,128)(2,1)S(1)} %bitcast_convert_fusion.1, bf16[1152,1152]{1,0:T(8,128)(2,1)S(1)} %copy-done, f32[384]{0:T(512)S(1)} %multiply_bitcast_fusion, ...), kind=kOutput, calls=%fused_computation.152 | convolution fusion | flops 1021869696 | bytes 7084032 | tf_op jit(solution)/shard_map/dot_general | solution.py:62
  74.6 1.7 %multiply_reduce_fusion.3 = (f32[384]{0:T(512)S(1)}, f32[1152,384]{0,1:T(8,128)S(1)}) fusion(f32[384]{0:T(512)S(1)} %multiply_add_fusion.3, f32[1152,384]{0,1:T(8,128)S(1)} %get-tuple-element.48, bf16[1152,1152]{1,0:T(8,128)(2,1)S(1)} %copy-done, f32[384]{0:T(512)S(1)} %multiply_bitcast_fusion, f32[384]{0:T(512)S(1)} %get-tuple-element.45), kind=kOutput, calls=%fused_computation.151 | convolution fusion | flops 1022312064 | bytes 6199296 | tf_op jit(solution)/shard_map/dot_general | solution.py:62
  76.3 2.7 %fusion.21 = f32[1152,384]{0,1:T(8,128)} fusion(f32[1152,384]{0,1:T(8,128)S(1)} %get-tuple-element.50, bf16[1152,1152]{1,0:T(8,128)(2,1)S(1)} %copy-done, f32[384]{0:T(512)S(1)} %multiply_add_fusion.2, f32[384]{0:T(512)S(1)} %multiply_bitcast_fusion, f32[384]{0:T(512)S(1)} %get-tuple-element.45), kind=kOutput, calls=%fused_computation.32 | convolution fusion | flops 1021427712 | bytes 6197760 | tf_op jit(solution)/shard_map/dot_general | solution.py:62
  79.1 2.8 %copy.7 = f32[1152,3,128]{2,0,1:T(8,128)} copy(f32[1152,3,128]{0,2,1:T(8,128)} %bitcast.73) | data formatting | bytes 3538944 | tf_op jit(solution)/shard_map/reshape | solution.py:67
  81.9 1.6 broadcast_multiply_fusion.1
  83.6 4.4 %collective-permute-start.6 = (f32[1152,1,128]{2,0,1:T(8,128)S(1)}, f32[1152,1,128]{2,0,1:T(8,128)S(1)}, u32[]{:S(2)}, u32[]{:S(2)}) collective-permute-start(f32[1152,1,128]{2,0,1:T(8,128)S(1)} %get-tuple-element.37), channel_id=1, source_target_pairs={{0,1},{1,2},{2,3},{3,4},{4,5},{5,6},{6,7},{7,8},{8,9},{9,10},{10,1... | collective-permute-start | bytes 1769480 | tf_op jit(solution)/shard_map/ppermute | solution.py:25
  88.0 1.9 %collective-permute-start.7 = (f32[1152,1,128]{2,0,1:T(8,128)S(1)}, f32[1152,1,128]{2,0,1:T(8,128)S(1)}, u32[]{:S(2)}, u32[]{:S(2)}) collective-permute-start(f32[1152,1,128]{2,0,1:T(8,128)S(1)} %get-tuple-element.38), channel_id=1, source_target_pairs={{1,0},{2,1},{3,2},{4,3},{5,4},{6,5},{7,6},{8,7},{9,8},{10,9},{11,1... | collective-permute-start | bytes 1769480 | tf_op jit(solution)/shard_map/ppermute | solution.py:26
  89.9 11.2 %collective-permute-done.6 = f32[1152,1,128]{2,0,1:T(8,128)S(1)} collective-permute-done((f32[1152,1,128]{2,0,1:T(8,128)S(1)}, f32[1152,1,128]{2,0,1:T(8,128)S(1)}, u32[]{:S(2)}, u32[]{:S(2)}) %collective-permute-start.6) | collective-permute-done | bytes 589856 | tf_op jit(solution)/shard_map/ppermute | solution.py:25
  101.3 1.0 fusion.122
  102.2 1.0 fusion.121
  103.2 2.1 %fusion.49 = f32[1152,3,128]{2,0,1:T(8,128)S(1)} fusion(f32[1152,1,128]{2,0,1:T(8,128)S(1)} %collective-permute-done.7, f32[1152,3,128]{2,0,1:T(8,128)S(1)} %broadcast_multiply_fusion.1, f32[1152,1,128]{2,0,1:T(8,128)S(1)} %collective-permute-done.6, f32[1152,5,1]{2,0,1:T(8,128)S(1)} %get-tuple-element.18, f32[1152,5,127]{2,0,1:T(8,128)S(1)} %get-tuple-element.20, ...), kind=kLoop, calls=%fused_computation.75 | loop fusion | flops 9289728 | bytes 12410880 | tf_op jit(solution)/shard_map/mul | solution.py:78
  105.4 4.4 %collective-permute-start.8 = (f32[1152,1,128]{2,0,1:T(8,128)S(1)}, f32[1152,1,128]{2,0,1:T(8,128)S(1)}, u32[]{:S(2)}, u32[]{:S(2)}) collective-permute-start(f32[1152,1,128]{2,0,1:T(8,128)S(1)} %get-tuple-element.35), channel_id=1, source_target_pairs={{0,1},{1,2},{2,3},{3,4},{4,5},{5,6},{6,7},{7,8},{8,9},{9,10},{10,1... | collective-permute-start | bytes 1769480 | tf_op jit(solution)/shard_map/ppermute | solution.py:25
  109.8 2.1 %collective-permute-start.9 = (f32[1152,1,128]{2,0,1:T(8,128)S(1)}, f32[1152,1,128]{2,0,1:T(8,128)S(1)}, u32[]{:S(2)}, u32[]{:S(2)}) collective-permute-start(f32[1152,1,128]{2,0,1:T(8,128)S(1)} %get-tuple-element.36), channel_id=1, source_target_pairs={{1,0},{2,1},{3,2},{4,3},{5,4},{6,5},{7,6},{8,7},{9,8},{10,9},{11,1... | collective-permute-start | bytes 1769480 | tf_op jit(solution)/shard_map/ppermute | solution.py:26
  111.9 11.0 %collective-permute-done.8 = f32[1152,1,128]{2,0,1:T(8,128)S(1)} collective-permute-done((f32[1152,1,128]{2,0,1:T(8,128)S(1)}, f32[1152,1,128]{2,0,1:T(8,128)S(1)}, u32[]{:S(2)}, u32[]{:S(2)}) %collective-permute-start.8) | collective-permute-done | bytes 589856 | tf_op jit(solution)/shard_map/ppermute | solution.py:25
  123.1 1.0 fusion.120
  125.0 2.1 %fusion.38 = f32[1152,3,128]{2,0,1:T(8,128)S(1)} fusion(f32[1152,1,128]{2,0,1:T(8,128)S(1)} %collective-permute-done.9, f32[1152,3,128]{2,0,1:T(8,128)S(1)} %fusion.49, f32[1152,1,128]{2,0,1:T(8,128)S(1)} %collective-permute-done.8, f32[1152,5,1]{2,0,1:T(8,128)S(1)} %get-tuple-element.14, f32[1152,5,127]{2,0,1:T(8,128)S(1)} %get-tuple-element.16, ...), kind=kLoop, calls=%fused_computation.57 | loop fusion | flops 9289728 | bytes 12410880 | tf_op jit(solution)/shard_map/mul | solution.py:78
  127.2 4.4 %collective-permute-start.10 = (f32[1152,1,128]{2,0,1:T(8,128)S(1)}, f32[1152,1,128]{2,0,1:T(8,128)S(1)}, u32[]{:S(2)}, u32[]{:S(2)}) collective-permute-start(f32[1152,1,128]{2,0,1:T(8,128)S(1)} %get-tuple-element.33), channel_id=1, source_target_pairs={{0,1},{1,2},{2,3},{3,4},{4,5},{5,6},{6,7},{7,8},{8,9},{9,10},{10,1... | collective-permute-start | bytes 1769480 | tf_op jit(solution)/shard_map/ppermute | solution.py:25
  131.6 1.9 %collective-permute-start.11 = (f32[1152,1,128]{2,0,1:T(8,128)S(1)}, f32[1152,1,128]{2,0,1:T(8,128)S(1)}, u32[]{:S(2)}, u32[]{:S(2)}) collective-permute-start(f32[1152,1,128]{2,0,1:T(8,128)S(1)} %get-tuple-element.34), channel_id=1, source_target_pairs={{1,0},{2,1},{3,2},{4,3},{5,4},{6,5},{7,6},{8,7},{9,8},{10,9},{11,1... | collective-permute-start | bytes 1769480 | tf_op jit(solution)/shard_map/ppermute | solution.py:26
  133.5 10.7 %collective-permute-done.10 = f32[1152,1,128]{2,0,1:T(8,128)S(1)} collective-permute-done((f32[1152,1,128]{2,0,1:T(8,128)S(1)}, f32[1152,1,128]{2,0,1:T(8,128)S(1)}, u32[]{:S(2)}, u32[]{:S(2)}) %collective-permute-start.10) | collective-permute-done | bytes 589856 | tf_op jit(solution)/shard_map/ppermute | solution.py:25
  146.3 3.0 %multiply_reduce_fusion.2 = (f32[3,128]{1,0:T(4,128)S(1)}, f32[1152,3,128]{2,0,1:T(8,128)}) fusion(f32[1152,1,128]{2,0,1:T(8,128)S(1)} %collective-permute-done.11, f32[1152,3,128]{2,0,1:T(8,128)S(1)} %fusion.38, f32[1152]{0:T(1024)S(1)} %get-tuple-element.55, f32[1152,1,128]{2,0,1:T(8,128)S(1)} %collective-permute-done.10, f32[1152]{0:T(1024)S(1)} %get-tuple-element.58, ...), kind=kLoop, calls=%fused_computation.150 | loop fusion | flops 10174080 | bytes 12412416 | tf_op jit(solution)/shard_map/reduce_sum | solution.py:63
  149.3 2.8 %copy.8 = f32[1152,3,128]{0,2,1:T(8,128)} copy(f32[1152,3,128]{2,0,1:T(8,128)} %get-tuple-element.6) | data formatting | bytes 3538944 | tf_op jit(solution)/shard_map/mul | solution.py:78
  152.1 1.7 %bitcast_convert_fusion = bf16[1152,384]{0,1:T(8,128)(2,1)S(1)} fusion(f32[1152,3,128]{0,2,1:T(8,128)} %copy.8), kind=kLoop, calls=%fused_computation.146 | loop fusion | flops 442368 | bytes 2654208 | tf_op jit(solution)/shard_map/convert_element_type | solution.py:61
  154.1 1.7 %multiply_reduce_fusion.1 = (f32[384]{0:T(512)S(1)}, f32[1152,384]{0,1:T(8,128)S(1)}) fusion(f32[384]{0:T(512)S(1)} %add_bitcast_fusion, f32[1152,384]{0,1:T(8,128)S(1)} %bitcast.71, bf16[1152,384]{0,1:T(8,128)(2,1)S(1)} %bitcast_convert_fusion, bf16[1152,1152]{1,0:T(8,128)(2,1)S(1)} %copy-done, f32[384]{0:T(512)S(1)} %multiply_bitcast_fusion, ...), kind=kOutput, calls=%fused_computation.149 | convolution fusion | flops 1021869696 | bytes 7084032 | tf_op jit(solution)/shard_map/dot_general | solution.py:62
  155.8 1.7 %multiply_reduce_fusion = (f32[384]{0:T(512)S(1)}, f32[1152,384]{0,1:T(8,128)S(1)}) fusion(f32[384]{0:T(512)S(1)} %multiply_add_fusion.1, f32[1152,384]{0,1:T(8,128)S(1)} %get-tuple-element.52, bf16[1152,1152]{1,0:T(8,128)(2,1)S(1)} %copy-done, f32[384]{0:T(512)S(1)} %multiply_bitcast_fusion, f32[384]{0:T(512)S(1)} %get-tuple-element.45), kind=kOutput, calls=%fused_computation.148 | convolution fusion | flops 1022312064 | bytes 6199296 | tf_op jit(solution)/shard_map/dot_general | solution.py:62
  157.6 2.7 %fusion.18 = f32[1152,384]{0,1:T(8,128)} fusion(f32[1152,384]{0,1:T(8,128)S(1)} %get-tuple-element.54, bf16[1152,1152]{1,0:T(8,128)(2,1)S(1)} %copy-done, f32[384]{0:T(512)S(1)} %multiply_add_fusion, f32[384]{0:T(512)S(1)} %multiply_bitcast_fusion, f32[384]{0:T(512)S(1)} %get-tuple-element.45), kind=kOutput, calls=%fused_computation.29 | convolution fusion | flops 1021427712 | bytes 6197760 | tf_op jit(solution)/shard_map/dot_general | solution.py:62
  160.3 2.8 %copy.9 = f32[1152,3,128]{2,0,1:T(8,128)} copy(f32[1152,3,128]{0,2,1:T(8,128)} %bitcast.72) | data formatting | bytes 3538944 | tf_op jit(solution)/shard_map/reshape | solution.py:67
  163.1 2.8 %broadcast_multiply_fusion = f32[1152,3,128]{2,0,1:T(8,128)} fusion(f32[1152,3,128]{2,0,1:T(8,128)} %copy.9, f32[3,128]{1,0:T(4,128)S(1)} %multiply_subtract_fusion), kind=kLoop, calls=%fused_computation.156 | loop fusion | flops 442368 | bytes 3540480 | tf_op jit(solution)/shard_map/mul | solution.py:79
  (48 shorter events, 5.3 us)
Async XLA Ops:
  0.0 72.6 %copy-start = (bf16[1152,1152]{1,0:T(8,128)(2,1)S(1)}, bf16[1152,1152]{1,0:T(8,128)(2,1)}, u32[]{:S(2)}) copy-start(bf16[1152,1152]{1,0:T(8,128)(2,1)} %param.9) | copy-start | bytes 7962628
  0.0 19.3 %copy-start.1 = (f32[1152,3,128]{2,0,1:T(8,128)S(1)}, f32[1152,3,128]{2,0,1:T(8,128)}, u32[]{:S(2)}) copy-start(f32[1152,3,128]{2,0,1:T(8,128)} %param.5) | copy-start | bytes 5308420
  0.0 8.2 %copy-start.4 = (s32[3,128]{1,0:T(4,128)S(1)}, s32[3,128]{1,0:T(4,128)}, u32[]{:S(2)}) copy-start(s32[3,128]{1,0:T(4,128)} %param.6) | copy-start | bytes 4612
  1.5 17.8 %collective-permute-start = (f32[1152,1,128]{2,0,1:T(8,128)S(1)}, f32[1152,1,128]{2,0,1:T(8,128)S(1)}, u32[]{:S(2)}, u32[]{:S(2)}) collective-permute-start(f32[1152,1,128]{2,0,1:T(8,128)S(1)} %get-tuple-element.43), channel_id=1, source_target_pairs={{0,1},{1,2},{2,3},{3,4},{4,5},{5,6},{6,7},{7,8},{8,9},{9,10},{10,1... | collective-permute-start | bytes 1769480 | tf_op jit(solution)/shard_map/ppermute | solution.py:25
  6.2 13.3 %collective-permute-start.1 = (f32[1152,1,128]{2,0,1:T(8,128)S(1)}, f32[1152,1,128]{2,0,1:T(8,128)S(1)}, u32[]{:S(2)}, u32[]{:S(2)}) collective-permute-start(f32[1152,1,128]{2,0,1:T(8,128)S(1)} %get-tuple-element.44), channel_id=1, source_target_pairs={{1,0},{2,1},{3,2},{4,3},{5,4},{6,5},{7,6},{8,7},{9,8},{10,9},{11,1... | collective-permute-start | bytes 1769480 | tf_op jit(solution)/shard_map/ppermute | solution.py:26
  23.6 17.5 %collective-permute-start.2 = (f32[1152,1,128]{2,0,1:T(8,128)S(1)}, f32[1152,1,128]{2,0,1:T(8,128)S(1)}, u32[]{:S(2)}, u32[]{:S(2)}) collective-permute-start(f32[1152,1,128]{2,0,1:T(8,128)S(1)} %get-tuple-element.41), channel_id=1, source_target_pairs={{0,1},{1,2},{2,3},{3,4},{4,5},{5,6},{6,7},{7,8},{8,9},{9,10},{10,1... | collective-permute-start | bytes 1769480 | tf_op jit(solution)/shard_map/ppermute | solution.py:25
  28.0 13.1 %collective-permute-start.3 = (f32[1152,1,128]{2,0,1:T(8,128)S(1)}, f32[1152,1,128]{2,0,1:T(8,128)S(1)}, u32[]{:S(2)}, u32[]{:S(2)}) collective-permute-start(f32[1152,1,128]{2,0,1:T(8,128)S(1)} %get-tuple-element.42), channel_id=1, source_target_pairs={{1,0},{2,1},{3,2},{4,3},{5,4},{6,5},{7,6},{8,7},{9,8},{10,9},{11,1... | collective-permute-start | bytes 1769480 | tf_op jit(solution)/shard_map/ppermute | solution.py:26
  45.4 6.6 %copy-start.5 = (f32[3,128]{1,0:T(4,128)S(1)}, f32[3,128]{1,0:T(4,128)}, u32[]{:S(2)}) copy-start(f32[3,128]{1,0:T(4,128)} %param.8) | copy-start | bytes 4612
  45.4 6.6 %copy-start.6 = (s32[3,128]{1,0:T(4,128)S(1)}, s32[3,128]{1,0:T(4,128)}, u32[]{:S(2)}) copy-start(s32[3,128]{1,0:T(4,128)} %param.7) | copy-start | bytes 4612
  45.5 17.5 %collective-permute-start.4 = (f32[1152,1,128]{2,0,1:T(8,128)S(1)}, f32[1152,1,128]{2,0,1:T(8,128)S(1)}, u32[]{:S(2)}, u32[]{:S(2)}) collective-permute-start(f32[1152,1,128]{2,0,1:T(8,128)S(1)} %get-tuple-element.39), channel_id=1, source_target_pairs={{0,1},{1,2},{2,3},{3,4},{4,5},{5,6},{6,7},{7,8},{8,9},{9,10},{10,1... | collective-permute-start | bytes 1769480 | tf_op jit(solution)/shard_map/ppermute | solution.py:25
  49.9 13.1 %collective-permute-start.5 = (f32[1152,1,128]{2,0,1:T(8,128)S(1)}, f32[1152,1,128]{2,0,1:T(8,128)S(1)}, u32[]{:S(2)}, u32[]{:S(2)}) collective-permute-start(f32[1152,1,128]{2,0,1:T(8,128)S(1)} %get-tuple-element.40), channel_id=1, source_target_pairs={{1,0},{2,1},{3,2},{4,3},{5,4},{6,5},{7,6},{8,7},{9,8},{10,9},{11,1... | collective-permute-start | bytes 1769480 | tf_op jit(solution)/shard_map/ppermute | solution.py:26
  70.9 2.0 %copy-start.2 = (f32[1152,3,128]{0,2,1:T(8,128)S(1)}, f32[1152,3,128]{0,2,1:T(8,128)}, u32[]{:S(2)}) copy-start(f32[1152,3,128]{0,2,1:T(8,128)} %copy.6) | copy-start | bytes 5308420
  83.6 17.5 %collective-permute-start.6 = (f32[1152,1,128]{2,0,1:T(8,128)S(1)}, f32[1152,1,128]{2,0,1:T(8,128)S(1)}, u32[]{:S(2)}, u32[]{:S(2)}) collective-permute-start(f32[1152,1,128]{2,0,1:T(8,128)S(1)} %get-tuple-element.37), channel_id=1, source_target_pairs={{0,1},{1,2},{2,3},{3,4},{4,5},{5,6},{6,7},{7,8},{8,9},{9,10},{10,1... | collective-permute-start | bytes 1769480 | tf_op jit(solution)/shard_map/ppermute | solution.py:25
  88.0 13.1 %collective-permute-start.7 = (f32[1152,1,128]{2,0,1:T(8,128)S(1)}, f32[1152,1,128]{2,0,1:T(8,128)S(1)}, u32[]{:S(2)}, u32[]{:S(2)}) collective-permute-start(f32[1152,1,128]{2,0,1:T(8,128)S(1)} %get-tuple-element.38), channel_id=1, source_target_pairs={{1,0},{2,1},{3,2},{4,3},{5,4},{6,5},{7,6},{8,7},{9,8},{10,9},{11,1... | collective-permute-start | bytes 1769480 | tf_op jit(solution)/shard_map/ppermute | solution.py:26
  105.4 17.5 %collective-permute-start.8 = (f32[1152,1,128]{2,0,1:T(8,128)S(1)}, f32[1152,1,128]{2,0,1:T(8,128)S(1)}, u32[]{:S(2)}, u32[]{:S(2)}) collective-permute-start(f32[1152,1,128]{2,0,1:T(8,128)S(1)} %get-tuple-element.35), channel_id=1, source_target_pairs={{0,1},{1,2},{2,3},{3,4},{4,5},{5,6},{6,7},{7,8},{8,9},{9,10},{10,1... | collective-permute-start | bytes 1769480 | tf_op jit(solution)/shard_map/ppermute | solution.py:25
  109.8 13.1 %collective-permute-start.9 = (f32[1152,1,128]{2,0,1:T(8,128)S(1)}, f32[1152,1,128]{2,0,1:T(8,128)S(1)}, u32[]{:S(2)}, u32[]{:S(2)}) collective-permute-start(f32[1152,1,128]{2,0,1:T(8,128)S(1)} %get-tuple-element.36), channel_id=1, source_target_pairs={{1,0},{2,1},{3,2},{4,3},{5,4},{6,5},{7,6},{8,7},{9,8},{10,9},{11,1... | collective-permute-start | bytes 1769480 | tf_op jit(solution)/shard_map/ppermute | solution.py:26
  127.2 17.0 %collective-permute-start.10 = (f32[1152,1,128]{2,0,1:T(8,128)S(1)}, f32[1152,1,128]{2,0,1:T(8,128)S(1)}, u32[]{:S(2)}, u32[]{:S(2)}) collective-permute-start(f32[1152,1,128]{2,0,1:T(8,128)S(1)} %get-tuple-element.33), channel_id=1, source_target_pairs={{0,1},{1,2},{2,3},{3,4},{4,5},{5,6},{6,7},{7,8},{8,9},{9,10},{10,1... | collective-permute-start | bytes 1769480 | tf_op jit(solution)/shard_map/ppermute | solution.py:25
  131.6 12.6 %collective-permute-start.11 = (f32[1152,1,128]{2,0,1:T(8,128)S(1)}, f32[1152,1,128]{2,0,1:T(8,128)S(1)}, u32[]{:S(2)}, u32[]{:S(2)}) collective-permute-start(f32[1152,1,128]{2,0,1:T(8,128)S(1)} %get-tuple-element.34), channel_id=1, source_target_pairs={{1,0},{2,1},{3,2},{4,3},{5,4},{6,5},{7,6},{8,7},{9,8},{10,9},{11,1... | collective-permute-start | bytes 1769480 | tf_op jit(solution)/shard_map/ppermute | solution.py:26
  152.1 2.0 %copy-start.3 = (f32[1152,3,128]{0,2,1:T(8,128)S(1)}, f32[1152,3,128]{0,2,1:T(8,128)}, u32[]{:S(2)}) copy-start(f32[1152,3,128]{0,2,1:T(8,128)} %copy.8) | copy-start | bytes 5308420
where the time goes:
time: 166 us
  waiting for transfers between devices  66 us (40%)
  starting transfers between devices  38.5 us (23%)
  local copies, waits for them, and re-layouts  25.3 us (15%)
  other arithmetic  23.3 us (14%)
  matrix products  12.3 us (7%)
    ppermute x6, waiting for transfers between devices, extended(): before = lax.ppermute(last, axis, up)  66 us
    ppermute x6, starting transfers between devices, extended(): before = lax.ppermute(last, axis, up)  26.6 us
    dot_general x6, matrix products, sources(): growth = jnp.dot(source_matrix, rounded, preferred_element_type=jnp.float32)  12.3 us
    ppermute x6, starting transfers between devices, extended(): after = lax.ppermute(leading, axis, down)  11.9 us
    slice x12, local copies, waits for them, and re-layouts, advance(): western = jnp.roll(spectra, 1, axis=2)  11.4 us
    mul x4, other arithmetic, on_device(): spectra = sea_local[None] * advance(widened, courant_x, courant_y)[:, 1:-1]  8.34 us
    reduce_sum x2, other arithmetic, sources(): energy = jnp.mean(flattened * flattened, axis=0, keepdims=True)  5.96 us
    reshape x2, local copies, waits for them, and re-layouts, sources(): return flattened.reshape(layout_shape)  5.6 us
  transfers between devices with their start and end apart: 12, of which 6 were waited for; matrix products, arithmetic and copies ran while one was open for 0% of the time, Pallas kernels for 0%

commit v1 on v0

v1 whole, which is shorter than its diff:
```python
import functools

import jax
import jax.numpy as jnp
import numpy as np
from jax import lax
from jax.experimental import pallas as pl
from jax.experimental.pallas import tpu as pltpu
from jax.sharding import PartitionSpec as P

NDIR = 36
NFREQ = 32
K = NDIR * NFREQ
STEPS = 2
SUBSTEPS = 3
SRC_SUB = 3
RATE = 0.5
DAMPING = 0.5

HALF = NDIR // 2
FREQS = 4
GROUP = FREQS * NDIR
SIDE = GROUP // 2
GROUPS = K // GROUP
BLOCK = 24
TILE = 288
MESH = pl.DeviceIdType.MESH


def packed_order():
    inside = np.arange(GROUP).reshape(FREQS, 2, HALF).transpose(1, 0, 2).reshape(-1)
    return inside, (np.arange(GROUPS)[:, None] * GROUP + inside).reshape(-1)


def coefficients(order):
    direction = (order % NDIR).astype(np.float32)
    frequency = (order // NDIR).astype(np.float32)
    angles = (2.0 * np.pi * (direction + 0.5) / NDIR).astype(np.float64)
    speeds = 0.6 * (0.35 + 0.65 * (NFREQ - 1 - frequency.astype(np.float64)) / (NFREQ - 1))
    cx, cy = speeds * np.cos(angles), speeds * np.sin(angles)
    cx, cy = cx.astype(np.float32), cy.astype(np.float32)
    staying = np.float32(1.0) - np.abs(cx) - np.abs(cy)
    return np.stack([staying, cx, np.abs(cy)], axis=1).astype(np.float32)


def pieces():
    for j in range(FREQS):
        for side in range(2):
            yield j * NDIR + side * HALF, side * SIDE + j * HALF


def kernel(size, spec, sea_ref, ice_ref, wind_ref, mat, coef_hbm, lanes_ref, subs_ref, out,
           nat, first, second, work, south, north, sea_south, sea_north, mat_nat, mat_packed, onehot,
           coef, low, total, load_sem, mat_sem, coef_sem, mask_send, mask_recv, up_send, up_recv,
           down_send, down_recv, out_sem):
    rows, width = spec.shape[0], spec.shape[2]
    me = lax.axis_index("comp")
    has_south, has_north = me > 0, me < size - 1

    loads = []
    for g in range(GROUPS):
        part = pl.ds(g * GROUP, GROUP)
        copy = pltpu.make_async_copy(spec.at[:, part, :], nat.at[:, part, :], load_sem.at[g])
        copy.start()
        loads.append(copy)
    mat_load = pltpu.make_async_copy(mat, mat_nat, mat_sem)
    mat_load.start()
    coef_load = pltpu.make_async_copy(coef_hbm, coef, coef_sem)
    coef_load.start()

    barrier = pltpu.get_barrier_semaphore()

    @pl.when(has_south)
    def _():
        pl.semaphore_signal(barrier, inc=1, device_id={"comp": me - 1}, device_id_type=MESH)

    @pl.when(has_north)
    def _():
        pl.semaphore_signal(barrier, inc=1, device_id={"comp": me + 1}, device_id_type=MESH)

    def up_copy(buffer, step, g):
        return pltpu.make_async_remote_copy(
            src_ref=buffer.at[pl.ds(rows - SUBSTEPS, SUBSTEPS), pl.ds(g * GROUP, SIDE), :],
            dst_ref=south.at[step, :, pl.ds(g * SIDE, SIDE), :],
            send_sem=up_send.at[step, g], recv_sem=up_recv.at[step, g],
            device_id={"comp": me + 1}, device_id_type=MESH)

    def down_copy(buffer, step, g):
        return pltpu.make_async_remote_copy(
            src_ref=buffer.at[pl.ds(0, SUBSTEPS), pl.ds(g * GROUP + SIDE, SIDE), :],
            dst_ref=north.at[step, :, pl.ds(g * SIDE, SIDE), :],
            send_sem=down_send.at[step, g], recv_sem=down_recv.at[step, g],
            device_id={"comp": me - 1}, device_id_type=MESH)

    def send(buffer, step, g):
        @pl.when(has_north)
        def _():
            up_copy(buffer, step, g).start()

        @pl.when(has_south)
        def _():
            down_copy(buffer, step, g).start()

    def mask_up():
        return pltpu.make_async_remote_copy(
            src_ref=sea_ref, dst_ref=sea_south, send_sem=mask_send.at[0], recv_sem=mask_recv.at[0],
            device_id={"comp": me + 1}, device_id_type=MESH)

    def mask_down():
        return pltpu.make_async_remote_copy(
            src_ref=sea_ref, dst_ref=sea_north, send_sem=mask_send.at[1], recv_sem=mask_recv.at[1],
            device_id={"comp": me - 1}, device_id_type=MESH)

    for g in range(GROUPS):
        loads[g].wait()
        for r in range(rows):
            for natural, packed in pieces():
                first[r, pl.ds(g * GROUP + packed, HALF), :] = nat[r, pl.ds(g * GROUP + natural, HALF), :]
        if g == 0:
            pl.semaphore_wait(barrier, has_south.astype(jnp.int32) + has_north.astype(jnp.int32))

            @pl.when(has_north)
            def _():
                mask_up().start()

            @pl.when(has_south)
            def _():
                mask_down().start()
        else:
            send(first, 0, g - 1)
    @pl.when(jnp.logical_not(has_south))
    def _():
        sea_south[...] = jnp.zeros_like(sea_south)
        south[...] = jnp.zeros_like(south)

    @pl.when(jnp.logical_not(has_north))
    def _():
        sea_north[...] = jnp.zeros_like(sea_north)
        north[...] = jnp.zeros_like(north)

    send(first, 0, GROUPS - 1)

    inner = (lax.broadcasted_iota(jnp.int32, (GROUP, GROUP), 1) == subs_ref[...])
    inner = inner.astype(jnp.float32).astype(jnp.bfloat16)

    def one_rows(i, carry):
        start = pl.multiple_of(i * GROUP, GROUP)
        line = lax.broadcasted_iota(jnp.int32, (GROUP, K), 0) + start
        onehot[pl.ds(start, GROUP), :] = (line == lanes_ref[...]).astype(jnp.float32).astype(jnp.bfloat16)
        return carry

    lax.fori_loop(0, GROUPS, one_rows, 0)
    mat_load.wait()
    third = K // 3

    def reorder(i, carry):
        start = pl.multiple_of(i * TILE, TILE)
        for c in range(3):
            columns = pl.ds(c * third, third)
            moved = jnp.dot(mat_nat[pl.ds(start, TILE), :], onehot[:, columns],
                            preferred_element_type=jnp.float32).astype(jnp.bfloat16)
            for s in range(TILE // GROUP):
                mat_packed[pl.ds(start + s * GROUP, GROUP), columns] = jnp.dot(
                    inner, moved[s * GROUP:(s + 1) * GROUP], preferred_element_type=jnp.float32
                ).astype(jnp.bfloat16)
        return carry

    lax.fori_loop(0, K // TILE, reorder, 0)
    coef_load.wait()

    @pl.when(has_south)
    def _():
        mask_up().wait_recv()

    @pl.when(has_north)
    def _():
        mask_down().wait_recv()

    sea = [sea_ref[pl.ds(r, 1), :].astype(jnp.float32) for r in range(rows)]
    sea_below = [sea_south[pl.ds(rows - SUBSTEPS + r, 1), :].astype(jnp.float32) for r in range(SUBSTEPS)]
    sea_above = [sea_north[pl.ds(r, 1), :].astype(jnp.float32) for r in range(SUBSTEPS)]
    thaw = [1.0 - 0.5 * ice_ref[pl.ds(r, 1), :].astype(jnp.float32) for r in range(rows)]
    gain = [RATE * wind_ref[pl.ds(r, 1), :] for r in range(rows)]

    def upwind(lines, seas, at):
        staying = coef[pl.ds(at, BLOCK), 0:1]
        cx = coef[pl.ds(at, BLOCK), 1:2]
        cy = jnp.broadcast_to(coef[pl.ds(at, BLOCK), 2:3], lines[0].shape)
        staying = jnp.broadcast_to(staying, lines[0].shape)
        cx = jnp.broadcast_to(cx, lines[0].shape)
        eastward, cx = cx > 0.0, jnp.abs(cx)
        for _ in range(SUBSTEPS):
            moved = []
            for i in range(1, len(lines)):
                side = jnp.where(eastward, pltpu.roll(lines[i], 1, 1), pltpu.roll(lines[i], width - 1, 1))
                moved.append(seas[i] * (staying * lines[i] + cx * side + cy * lines[i - 1]))
            lines, seas = moved, seas[1:]
        return lines

    def fold(value):
        return jnp.sum(value.reshape(-1, 8, width), axis=0)

    for step in range(STEPS):
        source = first if step == 0 else second
        for r in range(rows):
            total[r] = jnp.zeros((8, width), jnp.float32)
        for g in range(GROUPS):
            @pl.when(has_south)
            def _():
                up_copy(source, step, g).wait_recv()

            @pl.when(has_north)
            def _():
                down_copy(source, step, g).wait_recv()

            def block(i, carry):
                at = pl.multiple_of(g * GROUP + i * BLOCK, 8)
                halo = pl.multiple_of(g * SIDE + i * BLOCK, 8)
                lines = [south[step, r, pl.ds(halo, BLOCK), :] for r in range(SUBSTEPS)]
                lines += [source[r, pl.ds(at, BLOCK), :] for r in range(rows)]
                lines = upwind(lines, sea_below + sea, at)
                for r in range(rows):
                    work[r, pl.ds(at, BLOCK), :] = lines[r]
                at = pl.multiple_of(at + SIDE, 8)
                lines = [north[step, r, pl.ds(halo, BLOCK), :] for r in reversed(range(SUBSTEPS))]
                lines += [source[r, pl.ds(at, BLOCK), :] for r in reversed(range(rows))]
                lines = upwind(lines, (sea + sea_above)[::-1], at)
                for r in range(rows):
                    work[r, pl.ds(at, BLOCK), :] = lines[rows - 1 - r]
                return carry

            lax.fori_loop(0, SIDE // BLOCK, block, 0)
            for r in range(rows):
                value = work[r, pl.ds(g * GROUP, GROUP), :]
                low[0, pl.ds(g * GROUP, GROUP), pl.ds(r * width, width)] = value.astype(jnp.bfloat16)
                total[r] += fold(value * value)

        @pl.when(has_north)
        def _():
            for g in range(GROUPS):
                up_copy(source, step, g).wait_send()

        @pl.when(has_south)
        def _():
            for g in range(GROUPS):
                down_copy(source, step, g).wait_send()

        for sub in range(SRC_SUB):
            now, later = sub % 2, (sub + 1) % 2
            last = sub == SRC_SUB - 1
            scale = []
            for r in range(rows):
                energy = jnp.sum(total[r], axis=0, keepdims=True) * (1.0 / K)
                factor = sea[r] / (1.0 + DAMPING * energy)
                scale.append(factor * thaw[r] if last else factor)
                total[r] = jnp.zeros((8, width), jnp.float32)
            for t in range(K // TILE):
                part = pl.ds(t * TILE, TILE)
                growth = jnp.dot(mat_packed[part, :], low[now], preferred_element_type=jnp.float32)
                for r in range(rows):
                    value = (work[r, part, :] + gain[r] * growth[:, r * width:(r + 1) * width]) * scale[r]
                    if last:
                        second[r, part, :] = value
                    else:
                        work[r, part, :] = value
                        low[later, part, pl.ds(r * width, width)] = value.astype(jnp.bfloat16)
                        total[r] += fold(value * value)
                if last and step < STEPS - 1:
                    if t > 0:
                        for g in range((t - 1) * TILE // GROUP, t * TILE // GROUP):
                            send(second, step + 1, g)
                if last and step == STEPS - 1:
                    for g in range(t * TILE // GROUP, (t + 1) * TILE // GROUP):
                        for r in range(rows):
                            for natural, packed in pieces():
                                nat[r, pl.ds(g * GROUP + natural, HALF), :] = second[
                                    r, pl.ds(g * GROUP + packed, HALF), :]
                        area = pl.ds(g * GROUP, GROUP)
                        pltpu.make_async_copy(nat.at[:, area, :], out.at[:, area, :], out_sem.at[g]).start()
            if last and step < STEPS - 1:
                for g in range((K - TILE) // GROUP, GROUPS):
                    send(second, step + 1, g)
        if step == 0:
            @pl.when(has_north)
            def _():
                mask_up().wait_send()

            @pl.when(has_south)
            def _():
                mask_down().wait_send()

    for g in range(GROUPS):
        area = pl.ds(g * GROUP, GROUP)
        pltpu.make_async_copy(nat.at[:, area, :], out.at[:, area, :], out_sem.at[g]).wait()


def on_device(spectrum, sea_mask, ice_mask, wind, source_matrix):
    size = lax.axis_size("comp")
    spectra = spectrum.transpose(1, 0, 2)
    rows, _, width = spectra.shape
    inside, order = packed_order()
    coef = jnp.asarray(coefficients(order))
    lanes = jnp.asarray(order.astype(np.int32)[None, :])
    subs = jnp.asarray(inside.astype(np.int32)[:, None])
    hbm = pl.BlockSpec(memory_space=pl.ANY)
    vmem = pl.BlockSpec(memory_space=pltpu.VMEM)
    dma = pltpu.SemaphoreType.DMA
    full = pltpu.VMEM((rows, K, width), jnp.float32)
    result = pl.pallas_call(
        functools.partial(kernel, size),
        out_shape=jax.ShapeDtypeStruct(spectra.shape, jnp.float32),
        in_specs=[hbm, vmem, vmem, vmem, hbm, hbm, vmem, vmem],
        out_specs=hbm,
        scratch_shapes=[
            full, full, full, full,
            pltpu.VMEM((STEPS, SUBSTEPS, K // 2, width), jnp.float32),
            pltpu.VMEM((STEPS, SUBSTEPS, K // 2, width), jnp.float32),
            pltpu.VMEM(sea_mask.shape, jnp.int32),
            pltpu.VMEM(sea_mask.shape, jnp.int32),
            pltpu.VMEM((K, K), jnp.bfloat16),
            pltpu.VMEM((K, K), jnp.bfloat16),
            pltpu.VMEM((K, K), jnp.bfloat16),
            pltpu.VMEM(coef.shape, jnp.float32),
            pltpu.VMEM((2, K, rows * width), jnp.bfloat16),
            pltpu.VMEM((rows, 8, width), jnp.float32),
            dma((GROUPS,)), dma, dma, dma((2,)), dma((2,)),
            dma((STEPS, GROUPS)), dma((STEPS, GROUPS)), dma((STEPS, GROUPS)), dma((STEPS, GROUPS)),
            dma((GROUPS,)),
        ],
        compiler_params=pltpu.CompilerParams(
            collective_id=0, has_side_effects=True, vmem_limit_bytes=56 * 1024 * 1024),
        name="wave",
    )(spectra, sea_mask, ice_mask, wind, source_matrix, coef, lanes, subs)
    return result.transpose(1, 0, 2)


def solution(mesh):
    return jax.shard_map(
        on_device,
        mesh=mesh,
        in_specs=(
            P(None, ("grp", "comp"), None),
            P(("grp", "comp"), None),
            P(("grp", "comp"), None),
            P(("grp", "comp"), None),
            P(),
        ),
        out_specs=P(None, ("grp", "comp"), None),
        check_vma=False,
    )
```

time: 166 us -> 57.1 us (0.34)
  the two profiles are of different devices: /device:TPU:1 before, /device:TPU:20 now
where the time goes in v1:
time: 57.1 us; the launch traced here: 56.9 us
  Pallas kernels  54.1 us (95%)
  local copies, waits for them, and re-layouts  2.8 us (5%)
    pallas_call x1, Pallas kernels, on_device(): pl.pallas_call(functools.partial(kernel, size), out_shape=jax.ShapeDtypeS...  54.1 us
    unnamed x1, local copies, waits for them, and re-layouts  2.8 us

profile of v1, /device:TPU:20, one launch (start us, length us, event | category | flops | bytes accessed | tf_op | source)
XLA Modules:
  0.0 56.9 jit_solution(5433845304829855322)
XLA Ops:
  0.0 54.1 %wave.1 = f32[3,1152,128]{2,1,0:T(8,128)} custom-call(f32[3,1152,128]{2,1,0:T(8,128)} %bitcast.3, s32[3,128]{1,0:T(4,128)} %sea_ref.1, s32[3,128]{1,0:T(4,128)} %ice_ref.1, f32[3,128]{1,0:T(4,128)} %wind_ref.1, bf16[1152,1152]{1,0:T(8,128)(2,1)} %mat.1, f32[1152,3]{1,0:T(8,128)} %constant.6.clone.coef_hbm, s32[1,1152]{1,0:T(1,128)} %constant.7.clone.lanes_ref, ...), custom_call_target="tpu_custom_call" | custom-call | tf_op jit(solution)/shard_map/wave/pallas_call | solution.py:309
  54.1 2.8 %copy.10 = f32[1152,3,128]{2,0,1:T(8,128)} copy(f32[1152,3,128]{2,0,1:T(8,128)} %bitcast.2) | data formatting | bytes 3538944

commit v2 on v1

--- a/solution.py
+++ b/solution.py
@@ -51,7 +51,7 @@
 
 def kernel(size, spec, sea_ref, ice_ref, wind_ref, mat, coef_hbm, lanes_ref, subs_ref, out,
            nat, first, second, work, south, north, sea_south, sea_north, mat_nat, mat_packed, onehot,
-           coef, low, total, load_sem, mat_sem, coef_sem, mask_send, mask_recv, up_send, up_recv,
+           coef, low_middle, low_edges, last_rows, total, load_sem, mat_sem, coef_sem, mask_send, mask_recv, up_send, up_recv,
            down_send, down_recv, out_sem):
     rows, width = spec.shape[0], spec.shape[2]
     me = lax.axis_index("comp")
@@ -78,28 +78,38 @@
     def _():
         pl.semaphore_signal(barrier, inc=1, device_id={"comp": me + 1}, device_id_type=MESH)
 
-    def up_copy(buffer, step, g):
+    def up_copy(buffer, step, far, g):
         return pltpu.make_async_remote_copy(
-            src_ref=buffer.at[pl.ds(rows - SUBSTEPS, SUBSTEPS), pl.ds(g * GROUP, SIDE), :],
-            dst_ref=south.at[step, :, pl.ds(g * SIDE, SIDE), :],
-            send_sem=up_send.at[step, g], recv_sem=up_recv.at[step, g],
+            src_ref=buffer.at[rows - 1 - far, pl.ds(g * GROUP, SIDE), :],
+            dst_ref=south.at[step, SUBSTEPS - 1 - far, pl.ds(g * SIDE, SIDE), :],
+            send_sem=up_send.at[step, far, g], recv_sem=up_recv.at[step, far, g],
             device_id={"comp": me + 1}, device_id_type=MESH)
 
-    def down_copy(buffer, step, g):
+    def down_copy(buffer, step, far, g):
         return pltpu.make_async_remote_copy(
-            src_ref=buffer.at[pl.ds(0, SUBSTEPS), pl.ds(g * GROUP + SIDE, SIDE), :],
-            dst_ref=north.at[step, :, pl.ds(g * SIDE, SIDE), :],
-            send_sem=down_send.at[step, g], recv_sem=down_recv.at[step, g],
+            src_ref=buffer.at[far, pl.ds(g * GROUP + SIDE, SIDE), :],
+            dst_ref=north.at[step, far, pl.ds(g * SIDE, SIDE), :],
+            send_sem=down_send.at[step, far, g], recv_sem=down_recv.at[step, far, g],
             device_id={"comp": me - 1}, device_id_type=MESH)
 
-    def send(buffer, step, g):
+    def each(groups, act):
+        def once(i, carry):
+            act(groups[0] + i)
+            return carry
+
+        if len(groups) == 1:
+            act(groups[0])
+        else:
+            lax.fori_loop(0, len(groups), once, 0)
+
+    def send(buffer, step, far, groups):
         @pl.when(has_north)
         def _():
-            up_copy(buffer, step, g).start()
+            each(groups, lambda g: up_copy(buffer, step, far, g).start())
 
         @pl.when(has_south)
         def _():
-            down_copy(buffer, step, g).start()
+            each(groups, lambda g: down_copy(buffer, step, far, g).start())
 
     def mask_up():
         return pltpu.make_async_remote_copy(
@@ -127,7 +137,11 @@
             def _():
                 mask_down().start()
         else:
-            send(first, 0, g - 1)
+            send(first, 0, 0, (g - 1,))
+    send(first, 0, 0, (GROUPS - 1,))
+    for far in range(1, SUBSTEPS):
+        send(first, 0, far, range(GROUPS))
+
     @pl.when(jnp.logical_not(has_south))
     def _():
         sea_south[...] = jnp.zeros_like(sea_south)
@@ -137,8 +151,6 @@
     def _():
         sea_north[...] = jnp.zeros_like(sea_north)
         north[...] = jnp.zeros_like(north)
-
-    send(first, 0, GROUPS - 1)
 
     inner = (lax.broadcasted_iota(jnp.int32, (GROUP, GROUP), 1) == subs_ref[...])
     inner = inner.astype(jnp.float32).astype(jnp.bfloat16)
@@ -183,11 +195,10 @@
     gain = [RATE * wind_ref[pl.ds(r, 1), :] for r in range(rows)]
 
     def upwind(lines, seas, at):
-        staying = coef[pl.ds(at, BLOCK), 0:1]
-        cx = coef[pl.ds(at, BLOCK), 1:2]
-        cy = jnp.broadcast_to(coef[pl.ds(at, BLOCK), 2:3], lines[0].shape)
-        staying = jnp.broadcast_to(staying, lines[0].shape)
-        cx = jnp.broadcast_to(cx, lines[0].shape)
+        shape = lines[0].shape
+        staying = jnp.broadcast_to(coef[pl.ds(at, BLOCK), 0:1], shape)
+        cx = jnp.broadcast_to(coef[pl.ds(at, BLOCK), 1:2], shape)
+        cy = jnp.broadcast_to(coef[pl.ds(at, BLOCK), 2:3], shape)
         eastward, cx = cx > 0.0, jnp.abs(cx)
         for _ in range(SUBSTEPS):
             moved = []
@@ -195,103 +206,125 @@
                 side = jnp.where(eastward, pltpu.roll(lines[i], 1, 1), pltpu.roll(lines[i], width - 1, 1))
                 moved.append(seas[i] * (staying * lines[i] + cx * side + cy * lines[i - 1]))
             lines, seas = moved, seas[1:]
-        return lines
+        return lines[0]
 
     def fold(value):
         return jnp.sum(value.reshape(-1, 8, width), axis=0)
 
-    for step in range(STEPS):
-        source = first if step == 0 else second
-        for r in range(rows):
-            total[r] = jnp.zeros((8, width), jnp.float32)
-        for g in range(GROUPS):
+    def advance_rows(source, step, far):
+        upper, lower = rows - 1 - far, far
+        def group(g, carry):
             @pl.when(has_south)
             def _():
-                up_copy(source, step, g).wait_recv()
+                up_copy(source, step, far, g).wait_recv()
 
             @pl.when(has_north)
             def _():
-                down_copy(source, step, g).wait_recv()
-
-            def block(i, carry):
+                down_copy(source, step, far, g).wait_recv()
+
+            for i in range(SIDE // BLOCK):
                 at = pl.multiple_of(g * GROUP + i * BLOCK, 8)
                 halo = pl.multiple_of(g * SIDE + i * BLOCK, 8)
-                lines = [south[step, r, pl.ds(halo, BLOCK), :] for r in range(SUBSTEPS)]
-                lines += [source[r, pl.ds(at, BLOCK), :] for r in range(rows)]
-                lines = upwind(lines, sea_below + sea, at)
-                for r in range(rows):
-                    work[r, pl.ds(at, BLOCK), :] = lines[r]
+                lines = [south[step, SUBSTEPS - 1 - f, pl.ds(halo, BLOCK), :] for f in range(far, -1, -1)]
+                lines += [source[r, pl.ds(at, BLOCK), :] for r in range(upper + 1)]
+                seas = (sea_below + sea)[upper:upper + SUBSTEPS + 1]
+                work[upper, pl.ds(at, BLOCK), :] = upwind(lines, seas, at)
                 at = pl.multiple_of(at + SIDE, 8)
-                lines = [north[step, r, pl.ds(halo, BLOCK), :] for r in reversed(range(SUBSTEPS))]
-                lines += [source[r, pl.ds(at, BLOCK), :] for r in reversed(range(rows))]
-                lines = upwind(lines, (sea + sea_above)[::-1], at)
-                for r in range(rows):
-                    work[r, pl.ds(at, BLOCK), :] = lines[rows - 1 - r]
-                return carry
-
-            lax.fori_loop(0, SIDE // BLOCK, block, 0)
-            for r in range(rows):
-                value = work[r, pl.ds(g * GROUP, GROUP), :]
-                low[0, pl.ds(g * GROUP, GROUP), pl.ds(r * width, width)] = value.astype(jnp.bfloat16)
+                lines = [north[step, f, pl.ds(halo, BLOCK), :] for f in range(far, -1, -1)]
+                lines += [source[r, pl.ds(at, BLOCK), :] for r in range(rows - 1, lower - 1, -1)]
+                seas = (sea + sea_above)[lower:lower + SUBSTEPS + 1][::-1]
+                work[lower, pl.ds(at, BLOCK), :] = upwind(lines, seas, at)
+            return carry
+
+        lax.fori_loop(0, GROUPS, group, 0)
+
+    def prepare(chosen, low):
+        for j, r in enumerate(chosen):
+            total[r] = jnp.zeros((8, width), jnp.float32)
+            for t in range(K // TILE):
+                value = work[r, pl.ds(t * TILE, TILE), :]
+                low[0, pl.ds(t * TILE, TILE), pl.ds(j * width, width)] = value.astype(jnp.bfloat16)
                 total[r] += fold(value * value)
 
-        @pl.when(has_north)
-        def _():
-            for g in range(GROUPS):
-                up_copy(source, step, g).wait_send()
-
-        @pl.when(has_south)
-        def _():
-            for g in range(GROUPS):
-                down_copy(source, step, g).wait_send()
-
+    def grow(chosen, low, step, fars):
+        target = second if step < STEPS - 1 else last_rows
         for sub in range(SRC_SUB):
             now, later = sub % 2, (sub + 1) % 2
             last = sub == SRC_SUB - 1
-            scale = []
-            for r in range(rows):
+            scale = {}
+            for r in chosen:
                 energy = jnp.sum(total[r], axis=0, keepdims=True) * (1.0 / K)
                 factor = sea[r] / (1.0 + DAMPING * energy)
-                scale.append(factor * thaw[r] if last else factor)
+                scale[r] = factor * thaw[r] if last else factor
                 total[r] = jnp.zeros((8, width), jnp.float32)
-            for t in range(K // TILE):
-                part = pl.ds(t * TILE, TILE)
+            def tile(t):
+                part = pl.ds(pl.multiple_of(t * TILE, 16), TILE)
                 growth = jnp.dot(mat_packed[part, :], low[now], preferred_element_type=jnp.float32)
-                for r in range(rows):
-                    value = (work[r, part, :] + gain[r] * growth[:, r * width:(r + 1) * width]) * scale[r]
+                for j, r in enumerate(chosen):
+                    value = (work[r, part, :] + gain[r] * growth[:, j * width:(j + 1) * width]) * scale[r]
                     if last:
-                        second[r, part, :] = value
+                        target[r, part, :] = value
                     else:
                         work[r, part, :] = value
-                        low[later, part, pl.ds(r * width, width)] = value.astype(jnp.bfloat16)
+                        low[later, part, pl.ds(j * width, width)] = value.astype(jnp.bfloat16)
                         total[r] += fold(value * value)
+
+            if len(chosen) == 1:
+                each(range(K // TILE), tile)
                 if last and step < STEPS - 1:
-                    if t > 0:
-                        for g in range((t - 1) * TILE // GROUP, t * TILE // GROUP):
-                            send(second, step + 1, g)
-                if last and step == STEPS - 1:
-                    for g in range(t * TILE // GROUP, (t + 1) * TILE // GROUP):
-                        for r in range(rows):
-                            for natural, packed in pieces():
-                                nat[r, pl.ds(g * GROUP + natural, HALF), :] = second[
-                                    r, pl.ds(g * GROUP + packed, HALF), :]
-                        area = pl.ds(g * GROUP, GROUP)
-                        pltpu.make_async_copy(nat.at[:, area, :], out.at[:, area, :], out_sem.at[g]).start()
-            if last and step < STEPS - 1:
-                for g in range((K - TILE) // GROUP, GROUPS):
-                    send(second, step + 1, g)
-        if step == 0:
-            @pl.when(has_north)
-            def _():
-                mask_up().wait_send()
-
-            @pl.when(has_south)
-            def _():
-                mask_down().wait_send()
-
-    for g in range(GROUPS):
+                    send(second, step + 1, fars[0], range(GROUPS))
+            else:
+                for t in range(K // TILE):
+                    tile(t)
+                    if last and step < STEPS - 1 and t > 0:
+                        send(second, step + 1, fars[0], range((t - 1) * TILE // GROUP, t * TILE // GROUP))
+            if last and step == STEPS - 1:
+                each(range(GROUPS), lambda g: unpack(chosen, g))
+        if step < STEPS - 1 and len(chosen) > 1:
+            send(second, step + 1, fars[0], range((K - TILE) // GROUP, GROUPS))
+            send(second, step + 1, fars[1], range(GROUPS))
+
+    def unpack(chosen, g):
+        start = pl.multiple_of(g * GROUP, 8)
+        for r in chosen:
+            value = last_rows[r, pl.ds(start, GROUP), :]
+            nat[r, pl.ds(start, GROUP), :] = jnp.concatenate(
+                [value[packed:packed + HALF] for _, packed in pieces()], axis=0)
+            give(r, g).start()
+
+    def give(r, g):
         area = pl.ds(g * GROUP, GROUP)
-        pltpu.make_async_copy(nat.at[:, area, :], out.at[:, area, :], out_sem.at[g]).wait()
+        return pltpu.make_async_copy(nat.at[r, area, :], out.at[r, area, :], out_sem.at[r, g])
+
+    for step in range(STEPS):
+        source = first if step == 0 else second
+        advance_rows(source, step, 0)
+        advance_rows(source, step, 1)
+        middle, edges = [1], [0, rows - 1]
+        prepare(middle, low_middle)
+        grow(middle, low_middle, step, (1,))
+        advance_rows(source, step, 2)
+        prepare(edges, low_edges)
+        grow(edges, low_edges, step, (0, 2))
+
+    @pl.when(has_north)
+    def _():
+        mask_up().wait_send()
+        for step in range(STEPS):
+            for far in range(SUBSTEPS):
+                each(range(GROUPS), lambda g: up_copy(
+                    first if step == 0 else second, step, far, g).wait_send())
+
+    @pl.when(has_south)
+    def _():
+        mask_down().wait_send()
+        for step in range(STEPS):
+            for far in range(SUBSTEPS):
+                each(range(GROUPS), lambda g: down_copy(
+                    first if step == 0 else second, step, far, g).wait_send())
+
+    for r in range(rows):
+        each(range(GROUPS), lambda g: give(r, g).wait())
 
 
 def on_device(spectrum, sea_mask, ice_mask, wind, source_matrix):
@@ -305,6 +338,7 @@
     hbm = pl.BlockSpec(memory_space=pl.ANY)
     vmem = pl.BlockSpec(memory_space=pltpu.VMEM)
     dma = pltpu.SemaphoreType.DMA
+    link = dma((STEPS, SUBSTEPS, GROUPS))
     full = pltpu.VMEM((rows, K, width), jnp.float32)
     result = pl.pallas_call(
         functools.partial(kernel, size),
@@ -321,11 +355,13 @@
             pltpu.VMEM((K, K), jnp.bfloat16),
             pltpu.VMEM((K, K), jnp.bfloat16),
             pltpu.VMEM(coef.shape, jnp.float32),
-            pltpu.VMEM((2, K, rows * width), jnp.bfloat16),
+            pltpu.VMEM((2, K, width), jnp.bfloat16),
+            pltpu.VMEM((2, K, 2 * width), jnp.bfloat16),
+            full,
             pltpu.VMEM((rows, 8, width), jnp.float32),
             dma((GROUPS,)), dma, dma, dma((2,)), dma((2,)),
-            dma((STEPS, GROUPS)), dma((STEPS, GROUPS)), dma((STEPS, GROUPS)), dma((STEPS, GROUPS)),
-            dma((GROUPS,)),
+            link, link, link, link,
+            dma((rows, GROUPS)),
         ],
         compiler_params=pltpu.CompilerParams(
             collective_id=0, has_side_effects=True, vmem_limit_bytes=56 * 1024 * 1024),

time: 57.1 us -> 78.1 us (1.37)
  Pallas kernels: 54.1 us -> 75.1 us
    pallas_call x1, Pallas kernels: 54.1 us -> 75.1 us  [on_device(): pl.pallas_call(functools.partial(kernel, size), out_shape=jax.ShapeDtypeS...]
where the time goes in v2:
time: 78.1 us; the launch traced here: 77.9 us
  Pallas kernels  75.1 us (96%)
  local copies, waits for them, and re-layouts  2.8 us (4%)
    pallas_call x1, Pallas kernels, on_device(): pl.pallas_call(functools.partial(kernel, size), out_shape=jax.ShapeDtypeS...  75.1 us
    unnamed x1, local copies, waits for them, and re-layouts  2.8 us

profile of v2, /device:TPU:20, one launch (start us, length us, event | category | flops | bytes accessed | tf_op | source)
XLA Modules:
  0.0 77.9 jit_solution(6102061396026014511)
XLA Ops:
  0.0 75.1 %wave.1 = f32[3,1152,128]{2,1,0:T(8,128)} custom-call(f32[3,1152,128]{2,1,0:T(8,128)} %bitcast.3, s32[3,128]{1,0:T(4,128)} %sea_ref.1, s32[3,128]{1,0:T(4,128)} %ice_ref.1, f32[3,128]{1,0:T(4,128)} %wind_ref.1, bf16[1152,1152]{1,0:T(8,128)(2,1)} %mat.1, f32[1152,3]{1,0:T(8,128)} %constant.6.clone.coef_hbm, s32[1,1152]{1,0:T(1,128)} %constant.7.clone.lanes_ref, ...), custom_call_target="tpu_custom_call" | custom-call | tf_op jit(solution)/shard_map/wave/pallas_call | solution.py:343
  75.1 2.8 %copy.10 = f32[1152,3,128]{2,0,1:T(8,128)} copy(f32[1152,3,128]{2,0,1:T(8,128)} %bitcast.2) | data formatting | bytes 3538944

commit v3 on v1

--- a/solution.py
+++ b/solution.py
@@ -17,10 +17,11 @@
 RATE = 0.5
 DAMPING = 0.5
 
-HALF = NDIR // 2
-FREQS = 4
+QUARTER = NDIR // 4
+FREQS = 8
 GROUP = FREQS * NDIR
 SIDE = GROUP // 2
+PART = GROUP // 4
 GROUPS = K // GROUP
 BLOCK = 24
 TILE = 288
@@ -28,7 +29,7 @@
 
 
 def packed_order():
-    inside = np.arange(GROUP).reshape(FREQS, 2, HALF).transpose(1, 0, 2).reshape(-1)
+    inside = np.arange(GROUP).reshape(FREQS, 4, QUARTER).transpose(1, 0, 2).reshape(-1)
     return inside, (np.arange(GROUPS)[:, None] * GROUP + inside).reshape(-1)
 
 
@@ -40,13 +41,13 @@
     cx, cy = speeds * np.cos(angles), speeds * np.sin(angles)
     cx, cy = cx.astype(np.float32), cy.astype(np.float32)
     staying = np.float32(1.0) - np.abs(cx) - np.abs(cy)
-    return np.stack([staying, cx, np.abs(cy)], axis=1).astype(np.float32)
+    return np.stack([staying, np.abs(cx), np.abs(cy)], axis=1).astype(np.float32)
 
 
 def pieces():
     for j in range(FREQS):
-        for side in range(2):
-            yield j * NDIR + side * HALF, side * SIDE + j * HALF
+        for quarter in range(4):
+            yield j * NDIR + quarter * QUARTER, (quarter * FREQS + j) * QUARTER
 
 
 def kernel(size, spec, sea_ref, ice_ref, wind_ref, mat, coef_hbm, lanes_ref, subs_ref, out,
@@ -115,7 +116,7 @@
         loads[g].wait()
         for r in range(rows):
             for natural, packed in pieces():
-                first[r, pl.ds(g * GROUP + packed, HALF), :] = nat[r, pl.ds(g * GROUP + natural, HALF), :]
+                first[r, pl.ds(g * GROUP + packed, QUARTER), :] = nat[r, pl.ds(g * GROUP + natural, QUARTER), :]
         if g == 0:
             pl.semaphore_wait(barrier, has_south.astype(jnp.int32) + has_north.astype(jnp.int32))
 
@@ -182,17 +183,16 @@
     thaw = [1.0 - 0.5 * ice_ref[pl.ds(r, 1), :].astype(jnp.float32) for r in range(rows)]
     gain = [RATE * wind_ref[pl.ds(r, 1), :] for r in range(rows)]
 
-    def upwind(lines, seas, at):
+    def upwind(lines, seas, at, shift):
         staying = coef[pl.ds(at, BLOCK), 0:1]
         cx = coef[pl.ds(at, BLOCK), 1:2]
         cy = jnp.broadcast_to(coef[pl.ds(at, BLOCK), 2:3], lines[0].shape)
         staying = jnp.broadcast_to(staying, lines[0].shape)
         cx = jnp.broadcast_to(cx, lines[0].shape)
-        eastward, cx = cx > 0.0, jnp.abs(cx)
         for _ in range(SUBSTEPS):
             moved = []
             for i in range(1, len(lines)):
-                side = jnp.where(eastward, pltpu.roll(lines[i], 1, 1), pltpu.roll(lines[i], width - 1, 1))
+                side = pltpu.roll(lines[i], shift, 1)
                 moved.append(seas[i] * (staying * lines[i] + cx * side + cy * lines[i - 1]))
             lines, seas = moved, seas[1:]
         return lines
@@ -214,22 +214,25 @@
                 down_copy(source, step, g).wait_recv()
 
             def block(i, carry):
-                at = pl.multiple_of(g * GROUP + i * BLOCK, 8)
-                halo = pl.multiple_of(g * SIDE + i * BLOCK, 8)
-                lines = [south[step, r, pl.ds(halo, BLOCK), :] for r in range(SUBSTEPS)]
-                lines += [source[r, pl.ds(at, BLOCK), :] for r in range(rows)]
-                lines = upwind(lines, sea_below + sea, at)
-                for r in range(rows):
-                    work[r, pl.ds(at, BLOCK), :] = lines[r]
-                at = pl.multiple_of(at + SIDE, 8)
-                lines = [north[step, r, pl.ds(halo, BLOCK), :] for r in reversed(range(SUBSTEPS))]
-                lines += [source[r, pl.ds(at, BLOCK), :] for r in reversed(range(rows))]
-                lines = upwind(lines, (sea + sea_above)[::-1], at)
-                for r in range(rows):
-                    work[r, pl.ds(at, BLOCK), :] = lines[rows - 1 - r]
+                for quarter, shift in ((0, 1), (1, width - 1)):
+                    halo = pl.multiple_of(g * SIDE + quarter * PART + i * BLOCK, 8)
+                    at = pl.multiple_of(g * GROUP + quarter * PART + i * BLOCK, 8)
+                    lines = [south[step, r, pl.ds(halo, BLOCK), :] for r in range(SUBSTEPS)]
+                    lines += [source[r, pl.ds(at, BLOCK), :] for r in range(rows)]
+                    lines = upwind(lines, sea_below + sea, at, shift)
+                    for r in range(rows):
+                        work[r, pl.ds(at, BLOCK), :] = lines[r]
+                for quarter, shift in ((0, width - 1), (1, 1)):
+                    halo = pl.multiple_of(g * SIDE + quarter * PART + i * BLOCK, 8)
+                    at = pl.multiple_of(g * GROUP + SIDE + quarter * PART + i * BLOCK, 8)
+                    lines = [north[step, r, pl.ds(halo, BLOCK), :] for r in reversed(range(SUBSTEPS))]
+                    lines += [source[r, pl.ds(at, BLOCK), :] for r in reversed(range(rows))]
+                    lines = upwind(lines, (sea + sea_above)[::-1], at, shift)
+                    for r in range(rows):
+                        work[r, pl.ds(at, BLOCK), :] = lines[rows - 1 - r]
                 return carry
 
-            lax.fori_loop(0, SIDE // BLOCK, block, 0)
+            lax.fori_loop(0, PART // BLOCK, block, 0)
             for r in range(rows):
                 value = work[r, pl.ds(g * GROUP, GROUP), :]
                 low[0, pl.ds(g * GROUP, GROUP), pl.ds(r * width, width)] = value.astype(jnp.bfloat16)
@@ -273,8 +276,8 @@
                     for g in range(t * TILE // GROUP, (t + 1) * TILE // GROUP):
                         for r in range(rows):
                             for natural, packed in pieces():
-                                nat[r, pl.ds(g * GROUP + natural, HALF), :] = second[
-                                    r, pl.ds(g * GROUP + packed, HALF), :]
+                                nat[r, pl.ds(g * GROUP + natural, QUARTER), :] = second[
+                                    r, pl.ds(g * GROUP + packed, QUARTER), :]
                         area = pl.ds(g * GROUP, GROUP)
                         pltpu.make_async_copy(nat.at[:, area, :], out.at[:, area, :], out_sem.at[g]).start()
             if last and step < STEPS - 1:

time: 57.1 us -> 59.8 us (1.047)
  Pallas kernels: 54.1 us -> 56.8 us
    pallas_call x1, Pallas kernels: 54.1 us -> 56.8 us  [on_device(): pl.pallas_call(functools.partial(kernel, size), out_shape=jax.ShapeDtypeS...]
where the time goes in v3:
time: 59.8 us; the launch traced here: 59.6 us
  Pallas kernels  56.8 us (95%)
  local copies, waits for them, and re-layouts  2.8 us (5%)
    pallas_call x1, Pallas kernels, on_device(): pl.pallas_call(functools.partial(kernel, size), out_shape=jax.ShapeDtypeS...  56.8 us
    unnamed x1, local copies, waits for them, and re-layouts  2.8 us

profile of v3, /device:TPU:20, one launch (start us, length us, event | category | flops | bytes accessed | tf_op | source)
XLA Modules:
  0.0 59.6 jit_solution(665893423019770534)
XLA Ops:
  0.0 56.8 %wave.1 = f32[3,1152,128]{2,1,0:T(8,128)} custom-call(f32[3,1152,128]{2,1,0:T(8,128)} %bitcast.3, s32[3,128]{1,0:T(4,128)} %sea_ref.1, s32[3,128]{1,0:T(4,128)} %ice_ref.1, f32[3,128]{1,0:T(4,128)} %wind_ref.1, bf16[1152,1152]{1,0:T(8,128)(2,1)} %mat.1, f32[1152,3]{1,0:T(8,128)} %constant.6.clone.coef_hbm, s32[1,1152]{1,0:T(1,128)} %constant.7.clone.lanes_ref, ...), custom_call_target="tpu_custom_call" | custom-call | tf_op jit(solution)/shard_map/wave/pallas_call | solution.py:312
  56.8 2.8 %copy.10 = f32[1152,3,128]{2,0,1:T(8,128)} copy(f32[1152,3,128]{2,0,1:T(8,128)} %bitcast.2) | data formatting | bytes 3538944
